TPU v7x, 256 devices: a whole 4x4x8 slice. The times are simulated.
256 devices in a mesh: row: 8 (over z), col: 32 (over y, x, core).
Axes of the slice: x: 4, y: 4, z: 8, core: 2. Of those that a mesh axis runs over, the one named last changes fastest.
Arguments:
- panel_block: bfloat16 [28672, 1024], P(('row', 'col')), may hold values from -1.5 to 1.5
- diag_inverse: bfloat16 [2, 512, 512], replicated
- trailing: bfloat16 [28672, 28672], P('row', 'col'), may hold values from -6 to 6
Outputs:
- factor_panel: bfloat16 [28672, 1024], P(('row', 'col'))
- updated: bfloat16 [28672, 28672], P('row', 'col')
All inputs are finite; a program needn't handle non-finite values.
Results may differ from a plain program's by a relative error of at most 0.0054.
Values may be sent and summed in bfloat16 or wider, within the bound.
A program may use at most 128 MiB of HBM per device.

v0:
```python
import jax
import jax.numpy as jnp
from jax import lax
from jax.sharding import PartitionSpec as P

NB = 512
PANELS = 2


def sent_to_all(x, axis):
    peers = lax.axis_size(axis)
    return lax.all_to_all(jnp.broadcast_to(x[None], (peers, *x.shape)), axis, 0, 0, tiled=True)


def laid_out(pieces, dim):
    pieces = jnp.moveaxis(pieces, 0, dim)
    dims = pieces.shape
    return pieces.reshape(*dims[:dim], dims[dim] * dims[dim + 1], *dims[dim + 2 :])


def collect(x, axis, dim):
    pieces = sent_to_all(x, axis)
    return laid_out(pieces, dim)


def body(panel_block, diag_inverse, trailing):
    pieces = []
    for panel in range(PANELS):
        columns = panel_block[:, panel * NB : (panel + 1) * NB]
        pieces.append(
            jnp.dot(
                columns, jnp.tril(diag_inverse[panel]).T, preferred_element_type=jnp.float32
            ).astype(jnp.bfloat16)
        )
    factor = jnp.concatenate(pieces, axis=1)
    row_block = lax.all_gather(factor, "col", axis=0, tiled=True)
    product = lax.dot_general(
        row_block,
        collect(factor, "row", 0),
        (((1,), (1,)), ((), ())),
        preferred_element_type=jnp.float32,
    )
    updated = (trailing.astype(jnp.float32) - product).astype(jnp.bfloat16)
    return (factor, updated)


def solution(mesh):
    placed = (P(("row", "col"), None), P(), P("row", "col"))
    return jax.shard_map(
        body,
        mesh=mesh,
        in_specs=placed,
        out_specs=(P(("row", "col"), None), P("row", "col")),
        check_vma=False,
    )
```

profile of v0, /device:TPU:1, one launch (start us, length us, event | category | flops | bytes accessed | tf_op | source)
XLA Modules:
  0.0 91.9 jit_solution(386972775527290636)
XLA Ops:
  7.2 0.0 all-gather.2.cloned.1.call-start
  7.2 1.3 %fusion.1 = bf16[112,512]{1,0:T(8,128)(2,1)S(1)} fusion(bf16[2,512,512]{2,1,0:T(8,128)(2,1)} %param.4, bf16[112,1024]{1,0:T(8,128)(2,1)} %param.3), kind=kOutput, calls=%fused_computation.4 | convolution fusion | flops 59301888 | bytes 753664 | tf_op jit(solution)/shard_map/dot_general | solution.py:31
  8.6 1.3 %fusion = bf16[112,512]{1,0:T(8,128)(2,1)S(1)} fusion(bf16[2,512,512]{2,1,0:T(8,128)(2,1)} %param.4, bf16[112,1024]{1,0:T(8,128)(2,1)} %param.3), kind=kOutput, calls=%fused_computation.3 | convolution fusion | flops 59301888 | bytes 753664 | tf_op jit(solution)/shard_map/dot_general | solution.py:31
  9.9 0.7 pad_maximum_fusion
  10.6 0.0 all-gather.2.cloned.1.call-update
  10.6 1.2 %broadcast_in_dim.12 = bf16[8,112,1024]{2,1,0:T(8,128)(2,1)S(1)} broadcast(bf16[112,1024]{1,0:T(8,128)(2,1)} %pad_maximum_fusion), dimensions={1,2} | broadcast | bytes 2064384 | tf_op jit(solution)/shard_map/broadcast_in_dim | solution.py:12
  11.8 52.9 %all_to_all.5 = bf16[8,112,1024]{2,1,0:T(8,128)(2,1)S(1)} all-to-all(bf16[8,112,1024]{2,1,0:T(8,128)(2,1)S(1)} %broadcast_in_dim.12), channel_id=1, replica_groups=mesh['row'=8,'col'=32] {'row'}, dimensions={0} | all-to-all | bytes 3670016 | tf_op jit(solution)/shard_map/all_to_all | solution.py:12
  64.7 6.6 %all-gather.2.cloned.1.call-done = bf16[3584,1024]{1,0:T(8,128)(2,1)} async-done(((bf16[112,1024]{1,0:T(8,128)(2,1)}), bf16[3584,1024]{1,0:T(8,128)(2,1)}) %all-gather.2.cloned.1.call-update) | async-done | bytes 7340048 | tf_op jit(solution)/shard_map/all_gather | solution.py:36
  71.3 13.8 %subtract_convert_fusion = bf16[3584,896]{1,0:T(8,128)(2,1)} fusion(bf16[3584,896]{1,0:T(8,128)(2,1)} %param.5, bf16[3584,1024]{1,0:T(8,128)(2,1)} %all-gather.2.cloned.1.call-done, bf16[896,1024]{1,0:T(8,128)(2,1)S(1)} %bitcast.17), kind=kOutput, calls=%fused_computation | convolution fusion | flops 6586302464 | bytes 22020096 | tf_op jit(solution)/shard_map/dot_general | solution.py:37
Async XLA Ops:
  7.2 64.1 %all-gather.2.cloned.1.call-start = ((), (), s32[]{:S(2)}) async-start(), calls=%async_computation.1 | async-start | bytes 7569408 | tf_op jit(solution)/shard_map/all_gather | solution.py:36
Sparse Core Ops, SparseCore 0:
  11.1 60.0 all-gather.1
where the time goes:
time: 92.1 us; the launch traced here: 91.9 us
  blocking collectives  52.9 us (57%)
  matrix products  16.5 us (18%)
  between operations  14 us (15%)
  waiting for transfers between devices  6.57 us (7%)
  local copies, waits for them, and re-layouts  1.16 us (1%)
    all_to_all x1, blocking collectives, sent_to_all(): lax.all_to_all(jnp.broadcast_to(x[None], (peers, *x.shape)), axis, 0, 0,...  52.9 us
    dot_general x1, matrix products, body(): lax.dot_general(row_block, collect(factor, 'row', 0), (((1,), (1,)), ((),...  13.8 us
    all_gather x1, waiting for transfers between devices, body(): row_block = lax.all_gather(factor, 'col', axis=0, tiled=True)  6.55 us
    dot_general x2, matrix products, body(): jnp.dot(columns, jnp.tril(diag_inverse[panel]).T, preferred_element_type=...  2.68 us
  transfers between devices with their start and end apart: 1, of which 1 were waited for; matrix products, arithmetic and copies ran while one was open for 1% of the time, Pallas kernels for 0%

commit v1 on v0

--- a/solution.py
+++ b/solution.py
@@ -33,7 +33,9 @@
             ).astype(jnp.bfloat16)
         )
     factor = jnp.concatenate(pieces, axis=1)
-    row_block = lax.all_gather(factor, "col", axis=0, tiled=True)
+    row_block = jnp.concatenate(
+        lax.all_to_all(jnp.stack([factor] * lax.axis_size("col")), "col", 0, 0), axis=0
+    )
     product = lax.dot_general(
         row_block,
         collect(factor, "row", 0),

time: 92.1 us -> 162 us (1.76)
  blocking collectives: 52.9 us -> 147 us
  between operations: 14 us -> 0.7 us
  waiting for transfers between devices: 6.57 us -> 0 us
  matrix products: 16.5 us -> 12.4 us
    all_to_all x0 -> x1, blocking collectives: none -> 94.2 us  [body(): lax.all_to_all(jnp.stack([factor] * lax.axis_size('col')), 'col', 0, 0)]
    all_gather x1 -> x0, waiting for transfers between devices: 6.55 us -> none  [body(): row_block = lax.all_gather(factor, 'col', axis=0, tiled=True)]
    dot_general x1, matrix products: 13.8 us -> 9.72 us  [body(): lax.dot_general(row_block, collect(factor, 'row', 0), (((1,), (1,)), ((),...]
  transfers between devices with their start and end apart: 1 -> 0, of which waited for: 1 -> 0; matrix products, arithmetic and copies ran while one was open for 1% -> 0% of each run, Pallas kernels for 0% -> 0%
where the time goes in v1:
time: 162 us; the launch traced here: 161 us
  blocking collectives  147 us (91%)
  matrix products  12.4 us (8%)
    all_to_all x1, blocking collectives, body(): lax.all_to_all(jnp.stack([factor] * lax.axis_size('col')), 'col', 0, 0)  94.2 us
    all_to_all x1, blocking collectives, sent_to_all(): lax.all_to_all(jnp.broadcast_to(x[None], (peers, *x.shape)), axis, 0, 0,...  52.9 us
    dot_general x1, matrix products, body(): lax.dot_general(row_block, collect(factor, 'row', 0), (((1,), (1,)), ((),...  9.72 us

profile of v1, /device:TPU:1, one launch (start us, length us, event | category | flops | bytes accessed | tf_op | source)
XLA Modules:
  0.0 161.4 jit_solution(9618058536714888133)
XLA Ops:
  0.6 1.3 fusion
  2.0 1.3 fusion.1
  3.3 0.0 copy-start
  3.4 0.2 broadcast_in_dim.12
  3.6 52.9 %all_to_all.10 = bf16[8,112,1024]{2,1,0:T(8,128)(2,1)S(1)} all-to-all(bf16[8,112,1024]{2,1,0:T(8,128)(2,1)S(1)} %broadcast_in_dim.12), channel_id=1, replica_groups=mesh['row'=8,'col'=32] {'row'}, dimensions={0} | all-to-all | bytes 3670016 | tf_op jit(solution)/shard_map/all_to_all | solution.py:12
  56.5 0.0 slice-start
  56.5 0.9 stack.2
  57.4 0.0 copy-done
  57.4 0.0 slice-start.1
  57.4 94.2 %all_to_all.11 = bf16[32,112,1024]{2,1,0:T(8,128)(2,1)S(1)} all-to-all(bf16[32,112,1024]{2,1,0:T(8,128)(2,1)S(1)} %stack.2), channel_id=1, replica_groups=mesh['row'=8,'col'=32] {'col'}, dimensions={0} | all-to-all | bytes 14680064 | tf_op jit(solution)/shard_map/all_to_all | solution.py:37
  151.6 0.0 slice-done
  151.6 0.0 slice-done.1
  151.6 9.7 %subtract_convert_fusion = bf16[3584,896]{1,0:T(8,128)(2,1)} fusion(bf16[3584,896]{1,0:T(8,128)(2,1)S(1)} %bitcast.21, bf16[3584,1024]{1,0:T(8,128)(2,1)S(1)} %bitcast.18, bf16[896,1024]{1,0:T(8,128)(2,1)S(1)} %bitcast.19), kind=kOutput, calls=%fused_computation | convolution fusion | flops 6586302464 | bytes 22020096 | tf_op jit(solution)/shard_map/dot_general | solution.py:39
  (2 shorter events, 0.0 us)
Async XLA Ops:
  3.3 54.1 %copy-start = (bf16[112,1024]{1,0:T(8,128)(2,1)}, bf16[112,1024]{1,0:T(8,128)(2,1)S(1)}, u32[]{:S(2)}) copy-start(bf16[112,1024]{1,0:T(8,128)(2,1)S(1)} %pad_maximum_fusion) | copy-start | bytes 688132
  56.5 95.2 %slice-start = ((s8[6422528]{0:T(1024)(128)(4,1)}), s8[4194304]{0:T(1024)(128)(4,1)S(1)}, s32[]{:S(2)}) async-start(s8[6422528]{0:T(1024)(128)(4,1)} %bitcast.20), calls=%async_computation.2 | async-start | bytes 8388608
  57.4 94.2 %slice-start.1 = ((s8[6422528]{0:T(1024)(128)(4,1)}), s8[2228224]{0:T(1024)(128)(4,1)S(1)}, s32[]{:S(2)}) async-start(s8[6422528]{0:T(1024)(128)(4,1)} %bitcast.20), calls=%async_computation.3 | async-start | bytes 4456448
